TPU v7x, 32 devices: a whole 2x2x4 slice. The times are simulated.
32 devices in a mesh: dp: 8 (over z, y), tensor: 4 (over x, core).
Axes of the slice: x: 2, y: 2, z: 4, core: 2. Of those that a mesh axis runs over, the one named last changes fastest.
Arguments:
- block_input: bfloat16 [2048, 8, 768], P('tensor', 'dp'), may hold values from -6 to 6
- condition: bfloat16 [8, 128], P('dp'), may hold values from -6 to 6
- modulation_weight: bfloat16 [128, 4608], P(None, 'dp'), may hold values from -0.25 to 0.25
- modulation_bias: bfloat16 [4608], P('dp'), may hold values from -3 to 3
- first_gain: bfloat16 [768], P('dp'), may hold values from 0.5 to 1.5
- qkv_weight: bfloat16 [3, 768, 768], P(None, 'dp', 'tensor'), may hold values from -0.3125 to 0.3125
- out_weight: bfloat16 [768, 768], P('tensor', 'dp'), may hold values from -0.875 to 0.875
- second_gain: bfloat16 [768], P('dp'), may hold values from 0.5 to 1.5
- up_weight: bfloat16 [768, 3072], P('dp', 'tensor'), may hold values from -0.21875 to 0.21875
- up_bias: bfloat16 [3072], P('dp'), may hold values from -3 to 3
- down_weight: bfloat16 [3072, 768], P('tensor', 'dp'), may hold values from -0.109375 to 0.109375
- down_bias: bfloat16 [768], P('dp'), may hold values from -2 to 2
- grad_output: bfloat16 [2048, 8, 768], P('tensor', 'dp'), may hold values from -6 to 6
Outputs:
- block_output: bfloat16 [2048, 8, 768], P('tensor', 'dp')
- grad_input: float32 [2048, 8, 768], P('tensor', 'dp')
- grad_condition: float32 [8, 128], P('dp')
- grad_modulation_weight: float32 [128, 4608], replicated
- grad_modulation_bias: float32 [4608], replicated
- grad_first_gain: float32 [768], replicated
- grad_qkv_weight: float32 [3, 768, 768], P(None, 'dp', 'tensor')
- grad_out_weight: float32 [768, 768], P('tensor', 'dp')
- grad_second_gain: float32 [768], replicated
- grad_up_weight: float32 [768, 3072], P('dp', 'tensor')
- grad_up_bias: float32 [3072], replicated
- grad_down_weight: float32 [3072, 768], P('tensor', 'dp')
- grad_down_bias: float32 [768], replicated
- root_means: float32 [3], replicated
All inputs are finite; a program needn't handle non-finite values.
Results may differ from a plain program's by a relative error of at most 0.014.
The roundings to bfloat16 on the way count: a program that leaves them out, or rounds other values in their place, can miss the bound.
Values may be sent and summed in bfloat16 or wider, within the bound.
A program may use at most 128 MiB of HBM per device.

v0:
```python
from functools import partial
import jax
import jax.numpy as jnp
from jax import lax
from jax.sharding import PartitionSpec as P

HEAD_DIM = 64
PRECISE = lax.Precision.HIGHEST
EPSILON = 1e-05


def norm_mod(stream, gain_vec, shift_vec, scale_vec):
    row_mean = jnp.mean(stream, axis=-1, keepdims=True)
    centred = stream - row_mean
    variance = jnp.mean(centred * centred, axis=-1, keepdims=True)
    normed = centred * lax.rsqrt(variance + EPSILON) * gain_vec
    return normed * (1.0 + scale_vec) + shift_vec


def rotary_tables(length, head_width):
    half_dim = head_width // 2
    inverse = 1.0 / 10000.0 ** (jnp.arange(half_dim, dtype=jnp.float32) * 2.0 / head_width)
    angles = jnp.arange(length, dtype=jnp.float32)[:, None] * inverse[None, :]
    angles = jnp.concatenate([angles, angles], axis=-1)
    return (jnp.cos(angles), jnp.sin(angles))


def rotate(vector, cos_table, sine_table):
    half_dim = vector.shape[-1] // 2
    turned = jnp.concatenate([-vector[..., half_dim:], vector[..., :half_dim]], axis=-1)
    return vector * cos_table[:, None, None, :] + turned * sine_table[:, None, None, :]


def gelu_tanh(values):
    return jax.nn.gelu(values, approximate=True)


def seq_block(heads_all, sequence, offset, block_rows):
    whole_seq = lax.dynamic_index_in_dim(heads_all, sequence, 0, keepdims=False)
    return lax.dynamic_slice_in_dim(whole_seq, offset, block_rows, 1)


def blocks_to_rows(blocks, sequences, per_seq, length):
    heads_here, block_rows, head_width = (blocks.shape[1], blocks.shape[2], blocks.shape[3])
    arranged = blocks.reshape(sequences, per_seq, heads_here, block_rows, head_width).transpose(
        1, 3, 0, 2, 4
    )
    return arranged.reshape(length, sequences, heads_here, head_width)


def shards(
    block_input,
    condition,
    modulation_weight,
    modulation_bias,
    first_gain,
    qkv_weight,
    out_weight,
    second_gain,
    up_weight,
    up_bias,
    down_weight,
    down_bias,
    grad_output,
):
    n_tensor = lax.axis_size("tensor")
    n_data = lax.axis_size("dp")
    t_index = lax.axis_index("tensor")
    d_index = lax.axis_index("dp")
    local_rows, sequences, features = block_input.shape
    length = local_rows * n_tensor
    ada_full, ada_b_full, gain_one, qkv_w, out_w, gain_two, up_w, b_up_full, down_w, b_down_full = (
        lax.all_gather(modulation_weight, "dp", axis=1, tiled=True),
        lax.all_gather(modulation_bias, "dp", axis=0, tiled=True),
        lax.all_gather(first_gain, "dp", axis=0, tiled=True),
        lax.all_gather(qkv_weight, "dp", axis=1, tiled=True),
        lax.all_gather(out_weight, "dp", axis=1, tiled=True),
        lax.all_gather(second_gain, "dp", axis=0, tiled=True),
        lax.all_gather(up_weight, "dp", axis=0, tiled=True),
        lax.all_gather(up_bias, "dp", axis=0, tiled=True),
        lax.all_gather(down_weight, "dp", axis=1, tiled=True),
        lax.all_gather(down_bias, "dp", axis=0, tiled=True),
    )
    ada_float = ada_full.astype(jnp.float32)
    gain_one_f = gain_one.astype(jnp.float32)
    gain_two_f = gain_two.astype(jnp.float32)
    b_up_f = b_up_full.astype(jnp.float32)
    b_down_f = b_down_full.astype(jnp.float32)
    cond_float = condition.astype(jnp.float32)
    modulation = jnp.dot(cond_float, ada_float, precision=PRECISE) + ada_b_full.astype(jnp.float32)
    shift_attn, scale_attn, gate_attn, shift_mlp, scale_mlp, gate_mlp = jnp.split(
        modulation, 6, axis=-1
    )
    stream = block_input.astype(jnp.float32)
    attn_in = norm_mod(stream, gain_one_f, shift_attn, scale_attn).astype(jnp.bfloat16)
    full_attn_in = lax.all_gather(attn_in, "tensor", axis=0, tiled=True)
    projected = jnp.einsum("lbd,jde->lbje", full_attn_in, qkv_w, preferred_element_type=jnp.float32)
    heads_here = qkv_w.shape[2] // HEAD_DIM
    head_shape = (length, sequences, heads_here, HEAD_DIM)
    cos_table, sine_table = rotary_tables(length, HEAD_DIM)
    query_scale = HEAD_DIM ** (-0.5)
    query_pre = projected[:, :, 0].reshape(head_shape)
    key_pre = projected[:, :, 1].reshape(head_shape)
    query_rot = (rotate(query_pre, cos_table, sine_table) * query_scale).astype(jnp.bfloat16)
    key_rot = rotate(key_pre, cos_table, sine_table).astype(jnp.bfloat16)
    value_low = projected[:, :, 2].reshape(head_shape).astype(jnp.bfloat16)
    query_heads = query_rot.transpose(1, 2, 0, 3)
    key_heads = key_rot.transpose(1, 2, 0, 3)
    value_heads = value_low.transpose(1, 2, 0, 3)
    block_rows = min(512, length)
    per_seq = length // block_rows
    block_count = sequences * per_seq

    def forward_block(position):
        sequence = position // per_seq
        offset = position % per_seq * block_rows
        query_blk = seq_block(query_heads, sequence, offset, block_rows)
        key_seq = lax.dynamic_index_in_dim(key_heads, sequence, 0, keepdims=False)
        value_seq = lax.dynamic_index_in_dim(value_heads, sequence, 0, keepdims=False)
        scores = jnp.einsum("hqe,hke->hqk", query_blk, key_seq, preferred_element_type=jnp.float32)
        row_max = jnp.max(scores, axis=-1, keepdims=True)
        shifted = jnp.exp(scores - row_max)
        row_total = jnp.sum(shifted, axis=-1, keepdims=True)
        probs = (shifted / row_total).astype(jnp.bfloat16)
        mixed_blk = jnp.einsum("hqk,hke->hqe", probs, value_seq, preferred_element_type=jnp.float32)
        return (mixed_blk.astype(jnp.bfloat16), (row_max + jnp.log(row_total))[..., 0])

    mixed_blocks, log_total = lax.map(forward_block, jnp.arange(block_count))
    mixed_all = blocks_to_rows(mixed_blocks, sequences, per_seq, length).reshape(
        length, sequences, heads_here * HEAD_DIM
    )
    portion = mixed_all
    attn_out = lax.psum_scatter(
        jnp.einsum("lbe,ed->lbd", portion, out_w, preferred_element_type=jnp.float32),
        "tensor",
        scatter_dimension=0,
        tiled=True,
    )
    attn_branch = gate_attn * attn_out
    middle = stream + attn_branch
    mlp_in = norm_mod(middle, gain_two_f, shift_mlp, scale_mlp).astype(jnp.bfloat16)
    unit_count = up_w.shape[1]
    b_up_own = lax.dynamic_slice_in_dim(b_up_f, t_index * unit_count, unit_count, 0)
    full_mlp_in = lax.all_gather(mlp_in, "tensor", axis=0, tiled=True)
    hidden = (
        jnp.einsum("lbd,df->lbf", full_mlp_in, up_w, preferred_element_type=jnp.float32) + b_up_own
    )
    active = gelu_tanh(hidden).astype(jnp.bfloat16)
    portion = active
    mlp_out = (
        lax.psum_scatter(
            jnp.einsum("lbf,fd->lbd", portion, down_w, preferred_element_type=jnp.float32).astype(
                jnp.bfloat16
            ),
            "tensor",
            scatter_dimension=0,
            tiled=True,
        ).astype(jnp.float32)
        + b_down_f
    )
    mlp_branch = gate_mlp * mlp_out
    result = middle + mlp_branch
    local_squares = jnp.stack(
        [
            jnp.sum(attn_branch * attn_branch),
            jnp.sum(mlp_branch * mlp_branch),
            jnp.sum(result * result),
        ]
    )
    out_grad = grad_output.astype(jnp.float32)
    d_gate_mlp = jnp.sum(out_grad * mlp_out, axis=0)
    d_mlp = (gate_mlp * out_grad).astype(jnp.bfloat16)
    d_b_down = jnp.sum(d_mlp.astype(jnp.float32), axis=(0, 1))
    full_d_mlp = lax.all_gather(d_mlp, "tensor", axis=0, tiled=True)
    d_active = jnp.einsum("lbd,fd->lbf", full_d_mlp, down_w, preferred_element_type=jnp.float32)
    grad_down = jnp.einsum("lbf,lbd->fd", active, full_d_mlp, preferred_element_type=jnp.float32)
    d_hidden = jax.vjp(gelu_tanh, hidden)[1](d_active)[0].astype(jnp.bfloat16)
    grad_up = jnp.einsum("lbd,lbf->df", full_mlp_in, d_hidden, preferred_element_type=jnp.float32)
    own_b_up = jnp.sum(d_hidden.astype(jnp.float32), axis=(0, 1))
    d_b_up = lax.dynamic_update_slice_in_dim(
        jnp.zeros(b_up_f.shape, jnp.float32), own_b_up, t_index * unit_count, 0
    )
    portion = d_hidden
    d_mlp_in = lax.psum_scatter(
        jnp.einsum("lbf,df->lbd", portion, up_w, preferred_element_type=jnp.float32),
        "tensor",
        scatter_dimension=0,
        tiled=True,
    )
    pull_two = jax.vjp(norm_mod, middle, gain_two_f, shift_mlp, scale_mlp)[1]
    middle_part, d_gain_two, d_shift_mlp, d_scale_mlp = pull_two(d_mlp_in)
    d_middle = out_grad + middle_part
    d_gate_attn = jnp.sum(d_middle * attn_out, axis=0)
    d_attn = (gate_attn * d_middle).astype(jnp.bfloat16)
    full_d_attn = lax.all_gather(d_attn, "tensor", axis=0, tiled=True)
    grad_out = jnp.einsum("lbe,lbd->ed", mixed_all, full_d_attn, preferred_element_type=jnp.float32)
    d_mixed = jnp.einsum(
        "lbd,ed->lbe", full_d_attn, out_w, preferred_element_type=jnp.float32
    ).astype(jnp.bfloat16)
    d_mixed_heads = d_mixed.reshape(head_shape).transpose(1, 2, 0, 3)

    def backward_block(accums, inputs):
        key_acc, value_acc = accums
        position, log_blk = inputs
        sequence = position // per_seq
        offset = position % per_seq * block_rows
        query_blk = seq_block(query_heads, sequence, offset, block_rows)
        d_mixed_blk = seq_block(d_mixed_heads, sequence, offset, block_rows)
        key_seq = lax.dynamic_index_in_dim(key_heads, sequence, 0, keepdims=False)
        value_seq = lax.dynamic_index_in_dim(value_heads, sequence, 0, keepdims=False)
        scores = jnp.einsum("hqe,hke->hqk", query_blk, key_seq, preferred_element_type=jnp.float32)
        probs = jnp.exp(scores - log_blk[..., None])
        d_probs = jnp.einsum(
            "hqe,hke->hqk", d_mixed_blk, value_seq, preferred_element_type=jnp.float32
        )
        row_inner = jnp.sum(probs * d_probs, axis=-1, keepdims=True)
        d_scores = (probs * (d_probs - row_inner)).astype(jnp.bfloat16)
        d_query_blk = jnp.einsum(
            "hqk,hke->hqe", d_scores, key_seq, preferred_element_type=jnp.float32
        )
        d_key_blk = jnp.einsum(
            "hqk,hqe->hke", d_scores, query_blk, preferred_element_type=jnp.float32
        )
        d_value_blk = jnp.einsum(
            "hqk,hqe->hke",
            probs.astype(jnp.bfloat16),
            d_mixed_blk,
            preferred_element_type=jnp.float32,
        )
        key_now = lax.dynamic_index_in_dim(key_acc, sequence, 0, keepdims=False) + d_key_blk
        value_now = lax.dynamic_index_in_dim(value_acc, sequence, 0, keepdims=False) + d_value_blk
        key_acc = lax.dynamic_update_index_in_dim(key_acc, key_now, sequence, 0)
        value_acc = lax.dynamic_update_index_in_dim(value_acc, value_now, sequence, 0)
        return ((key_acc, value_acc), d_query_blk)

    zero_heads = jnp.zeros((sequences, heads_here, length, HEAD_DIM), jnp.float32)
    (d_key_heads, d_value_heads), d_query_blocks = lax.scan(
        backward_block, (zero_heads, zero_heads), (jnp.arange(block_count), log_total)
    )
    d_query_rot = blocks_to_rows(d_query_blocks, sequences, per_seq, length) * query_scale
    pull_rotate = jax.vjp(partial(rotate, cos_table=cos_table, sine_table=sine_table), query_pre)[1]
    d_query_pre = pull_rotate(d_query_rot)[0]
    d_key_pre = pull_rotate(d_key_heads.transpose(2, 0, 1, 3))[0]
    d_value_all = d_value_heads.transpose(2, 0, 1, 3)
    flat_shape = (length, sequences, heads_here * HEAD_DIM)
    d_projected = jnp.stack(
        [
            d_query_pre.reshape(flat_shape),
            d_key_pre.reshape(flat_shape),
            d_value_all.reshape(flat_shape),
        ],
        axis=2,
    ).astype(jnp.bfloat16)
    grad_qkv = jnp.einsum(
        "lbd,lbje->jde", full_attn_in, d_projected, preferred_element_type=jnp.float32
    )
    portion = d_projected
    d_attn_in = lax.psum_scatter(
        jnp.einsum("lbje,jde->lbd", portion, qkv_w, preferred_element_type=jnp.float32),
        "tensor",
        scatter_dimension=0,
        tiled=True,
    )
    pull_one = jax.vjp(norm_mod, stream, gain_one_f, shift_attn, scale_attn)[1]
    stream_part, d_gain_one, d_shift_attn, d_scale_attn = pull_one(d_attn_in)
    d_stream = d_middle + stream_part
    grad_qkv_own, grad_out_own, grad_up_own, grad_down_own = (
        lax.psum_scatter(grad_qkv, "dp", scatter_dimension=1, tiled=True),
        lax.psum_scatter(grad_out, "dp", scatter_dimension=1, tiled=True),
        lax.psum_scatter(grad_up, "dp", scatter_dimension=0, tiled=True),
        lax.psum_scatter(grad_down, "dp", scatter_dimension=1, tiled=True),
    )
    d_modulation = jnp.concatenate(
        [d_shift_attn, d_scale_attn, d_gate_attn, d_shift_mlp, d_scale_mlp, d_gate_mlp], axis=-1
    )
    d_ada_b = jnp.sum(d_modulation, axis=0)
    d_ada_w = jnp.dot(cond_float.T, d_modulation, precision=PRECISE)
    d_cond_here = jnp.dot(d_modulation, ada_float.T, precision=PRECISE)
    cond_table = jnp.zeros((sequences * n_data, condition.shape[1]), jnp.float32)
    cond_table = lax.dynamic_update_slice_in_dim(cond_table, d_cond_here, d_index * sequences, 0)
    totals = lax.psum(
        (local_squares, cond_table, d_ada_w, d_ada_b, d_gain_one, d_gain_two, d_b_up, d_b_down),
        ("dp", "tensor"),
    )
    root_means = jnp.sqrt(totals[0] / (local_rows * sequences * features * n_tensor * n_data))
    grad_condition = lax.dynamic_slice_in_dim(totals[1], d_index * sequences, sequences, 0)
    return (
        result.astype(jnp.bfloat16),
        d_stream,
        grad_condition,
        totals[2],
        totals[3],
        totals[4],
        grad_qkv_own,
        grad_out_own,
        totals[5],
        grad_up_own,
        totals[6],
        grad_down_own,
        totals[7],
        root_means,
    )


def solution(mesh):
    in_specs = (
        P("tensor", "dp", None),
        P("dp", None),
        P(None, "dp"),
        P("dp"),
        P("dp"),
        P(None, "dp", "tensor"),
        P("tensor", "dp"),
        P("dp"),
        P("dp", "tensor"),
        P("dp"),
        P("tensor", "dp"),
        P("dp"),
        P("tensor", "dp", None),
    )
    out_specs = (
        P("tensor", "dp", None),
        P("tensor", "dp", None),
        P("dp", None),
        P(),
        P(),
        P(),
        P(None, "dp", "tensor"),
        P("tensor", "dp"),
        P(),
        P("dp", "tensor"),
        P(),
        P("tensor", "dp"),
        P(),
        P(),
    )
    return jax.shard_map(shards, mesh=mesh, in_specs=in_specs, out_specs=out_specs, check_vma=False)
```

profile of v0, /device:TPU:0, one launch (start us, length us, event | category | flops | bytes accessed | tf_op | source)
XLA Modules:
  0.0 1209.0 jit_solution(3161789117916995180)
XLA Ops:
  13.9 39.8 %all-reduce.9 = (bf16[4608]{0:T(1024)(128)(2,1)S(1)}, bf16[768]{0:T(1024)(128)(2,1)S(1)}, bf16[768]{0:T(1024)(128)(2,1)}, bf16[768]{0:T(1024)(128)(2,1)}) all-reduce(bf16[4608]{0:T(1024)(128)(2,1)S(1)} %dynamic-update-slice, bf16[768]{0:T(1024)(128)(2,1)S(1)} %dynamic-update-slice.1, ...), channel_id=1, replica_groups=mesh['dp'=8,'tensor'=4] {'dp'}, use_global_device_ids=true, to_apply=%add.4 | all-reduce | flops 6912 | bytes 27648
  60.7 34.8 %all_gather.46 = bf16[3,768,192]{2,0,1:T(4,128)(2,1)S(1)} all-gather(bf16[3,96,192]{2,0,1:T(4,128)(2,1)S(1)} %copy.49), channel_id=1, replica_groups=mesh['dp'=8,'tensor'=4] {'dp'}, dimensions={1}, use_global_device_ids=true | all-gather | bytes 995328 | tf_op jit(solution)/shard_map/all_gather | solution.py:76
  97.6 33.3 %all_gather.47 = bf16[192,768]{0,1:T(8,128)(2,1)} all-gather(bf16[192,96]{0,1:T(8,128)(2,1)S(1)} %copy.55), channel_id=1, replica_groups=mesh['dp'=8,'tensor'=4] {'dp'}, dimensions={1}, use_global_device_ids=true | all-gather | bytes 331776 | tf_op jit(solution)/shard_map/all_gather | solution.py:77
  146.7 101.9 %while.30 = (s32[]{:T(128)}, bf16[4,3,512,64]{3,2,1,0:T(8,128)(2,1)}, f32[4,3,512]{2,1,0:T(4,128)}, s32[4]{0:T(128)S(1)}, bf16[1,3,2048,64]{2,3,1,0:T(8,128)(2,1...) while((s32[]{:T(128)}, ...), condition=%wide.region_5.6_spmd, body=%wide.region_2.5_spmd.sunk | while | flops 1217493504 | bytes 29923640 | solution.py:128
  151.1 14.6 %dot_general.129 = f32[3,512,64]{2,1,0:T(8,128)} custom-call(bf16[3,512,64]{2,1,0:T(8,128)(2,1)} %bitcast.231, bf16[3,2048,64]{2,1,0:T(8,128)(2,1)S(1)} %bitcast.227, bf16[3,2048,64]{2,1,0:T(8,128)(2,1)} %bitcast.230), custom_call_target="tpu_custom_call" | custom-call | flops 805306368 | bytes 1769472 | tf_op jit(solution)/shard_map/while/body/eval_jaxpr/hqk,hke->hqe/dot_general | solution.py:125
  176.6 14.7 %dot_general.129 = f32[3,512,64]{2,1,0:T(8,128)} custom-call(bf16[3,512,64]{2,1,0:T(8,128)(2,1)} %bitcast.231, bf16[3,2048,64]{2,1,0:T(8,128)(2,1)S(1)} %bitcast.227, bf16[3,2048,64]{2,1,0:T(8,128)(2,1)} %bitcast.230), custom_call_target="tpu_custom_call" | custom-call | flops 805306368 | bytes 1769472 | tf_op jit(solution)/shard_map/while/body/eval_jaxpr/hqk,hke->hqe/dot_general | solution.py:125
  202.1 14.7 %dot_general.129 = f32[3,512,64]{2,1,0:T(8,128)} custom-call(bf16[3,512,64]{2,1,0:T(8,128)(2,1)} %bitcast.231, bf16[3,2048,64]{2,1,0:T(8,128)(2,1)S(1)} %bitcast.227, bf16[3,2048,64]{2,1,0:T(8,128)(2,1)} %bitcast.230), custom_call_target="tpu_custom_call" | custom-call | flops 805306368 | bytes 1769472 | tf_op jit(solution)/shard_map/while/body/eval_jaxpr/hqk,hke->hqe/dot_general | solution.py:125
  227.5 14.7 %dot_general.129 = f32[3,512,64]{2,1,0:T(8,128)} custom-call(bf16[3,512,64]{2,1,0:T(8,128)(2,1)} %bitcast.231, bf16[3,2048,64]{2,1,0:T(8,128)(2,1)S(1)} %bitcast.227, bf16[3,2048,64]{2,1,0:T(8,128)(2,1)} %bitcast.230), custom_call_target="tpu_custom_call" | custom-call | flops 805306368 | bytes 1769472 | tf_op jit(solution)/shard_map/while/body/eval_jaxpr/hqk,hke->hqe/dot_general | solution.py:125
  256.4 56.3 %reduce-scatter.13.cloned.1.call-done = f32[512,1,768]{2,0,1:T(8,128)} async-done(((f32[2048,1,768]{2,0,1:T(8,128)}), f32[512,1,768]{2,0,1:T(8,128)}) %reduce-scatter.13.cloned.1.call-update) | async-done | bytes 1572880 | tf_op jit(solution)/shard_map/reduce_scatter | solution.py:133
  319.7 26.1 %all-gather = bf16[8,1,384]{2,1,0:T(2,128)(2,1)S(1)} all-gather(bf16[1,1,384]{2,1,0:T(2,128)(2,1)S(1)} %reshape.555), channel_id=1, replica_groups=mesh['dp'=8,'tensor'=4] {'dp'}, dimensions={0}, use_global_device_ids=true | all-gather | bytes 6912 | tf_op jit(solution)/shard_map/all_gather | solution.py:80
  356.1 29.4 %all-gather.13.cloned.1.call-done = bf16[2048,1,768]{2,0,1:T(8,128)(2,1)} async-done(((bf16[512,1,768]{2,0,1:T(8,128)(2,1)}), bf16[2048,1,768]{2,0,1:T(8,128)(2,1)}) %all-gather.13.cloned.1.call-update) | async-done | bytes 3145744 | tf_op jit(solution)/shard_map/all_gather | solution.py:144
  393.0 35.9 %all-gather.17.cloned.1.call-done = bf16[768,768]{0,1:T(8,128)(2,1)} async-done(((bf16[768,96]{0,1:T(8,128)(2,1)}), bf16[768,768]{0,1:T(8,128)(2,1)}) %all-gather.17.cloned.1.call-update) | async-done | bytes 1179664 | tf_op jit(solution)/shard_map/all_gather | solution.py:81
  437.9 20.6 %all-gather.19.cloned.1.call-done = bf16[2048,1,768]{2,0,1:T(8,128)(2,1)} async-done(((bf16[512,1,768]{2,0,1:T(8,128)(2,1)}), bf16[2048,1,768]{2,0,1:T(8,128)(2,1)}) %all-gather.19.cloned.1.call-update) | async-done | bytes 3145744 | tf_op jit(solution)/shard_map/all_gather | solution.py:174
  475.6 23.6 %reduce-scatter.15.cloned.1.call-done = bf16[512,1,768]{2,0,1:T(8,128)(2,1)} async-done(((bf16[2048,1,768]{2,0,1:T(8,128)(2,1)}), bf16[512,1,768]{2,0,1:T(8,128)(2,1)}) %reduce-scatter.15.cloned.1.call-update) | async-done | bytes 786448 | tf_op jit(solution)/shard_map/reduce_scatter | solution.py:151
  499.1 60.9 %reduce-scatter.17.cloned.1.call-done = f32[512,1,768]{2,0,1:T(8,128)} async-done(((f32[2048,1,768]{2,0,1:T(8,128)}), f32[512,1,768]{2,0,1:T(8,128)}) %reduce-scatter.17.cloned.1.call-update) | async-done | bytes 1572880 | tf_op jit(solution)/shard_map/reduce_scatter | solution.py:184
  569.5 28.6 %all-gather.21.cloned.1.call-done = bf16[2048,1,768]{2,0,1:T(8,128)(2,1)} async-done(((bf16[512,1,768]{2,0,1:T(8,128)(2,1)}), bf16[2048,1,768]{2,0,1:T(8,128)(2,1)}) %all-gather.21.cloned.1.call-update) | async-done | bytes 3145744 | tf_op jit(solution)/shard_map/all_gather | solution.py:195
  603.6 110.1 %while.31 = (s32[]{:T(128)}, f32[1,3,2048,64]{2,3,1,0:T(8,128)S(1)}, f32[1,3,2048,64]{2,3,1,0:T(8,128)}, f32[4,3,512,64]{2,3,1,0:T(8,128)}, s32[4]{0:T(128)S(1)}...) while((s32[]{:T(128)}, ...), condition=%wide.region_15.16_spmd, body=%wide.region_13.15_spmd.sunk | while | flops 2042362368 | bytes 129411448 | solution.py:237
  764.0 19.5 %reduce-scatter.27.cloned.1.call-done = f32[96,192]{1,0:T(8,128)} async-done(((f32[768,192]{1,0:T(8,128)}), f32[96,192]{1,0:T(8,128)}) %reduce-scatter.27.cloned.1.call-update) | async-done | bytes 73744
  785.1 68.1 %reduce-scatter.25.cloned.1.call-done = f32[96,576]{1,0:T(8,128)} async-done(((f32[768,576]{1,0:T(8,128)}), f32[96,576]{1,0:T(8,128)}) %reduce-scatter.25.cloned.1.call-update) | async-done | bytes 221200
  855.2 58.1 %reduce-scatter.19.cloned.1.call-done = f32[512,1,768]{2,0,1:T(8,128)} async-done(((f32[2048,1,768]{2,0,1:T(8,128)}), f32[512,1,768]{2,0,1:T(8,128)}) %reduce-scatter.19.cloned.1.call-update) | async-done | bytes 1572880 | tf_op jit(solution)/shard_map/reduce_scatter | solution.py:258
  925.0 41.4 %all-reduce.8 = (f32[8,128]{1,0:T(8,128)S(1)}, f32[4608]{0:T(1024)}, f32[768]{0:T(1024)}, f32[768]{0:T(1024)}, f32[3072]{0:T(1024)}, /*index=5*/f32[768]{0:T(1024)}, f32[3]{0:T(128)S(1)}) all-reduce(f32[8,128]{1,0:T(8,128)S(1)} %dynamic_update_slice.30, f32[4608]{0:T(1024)S(1)} %reduce.25, ...), channel_id=1, replica_groups=mesh['dp'=8,'tensor'=4] {'dp','tensor'}, use_global_device_ids=true, to_apply=%region_25.26 | all-reduce | flops 11011 | bytes 88088 | tf_op jit(solution)/shard_map/psum | solution.py:281
  967.4 19.2 %reduce-scatter.23.cloned.1.call-done = f32[768,96]{0,1:T(8,128)} async-done(((f32[768,768]{0,1:T(8,128)}), f32[768,96]{0,1:T(8,128)}) %reduce-scatter.23.cloned.1.call-update) | async-done | bytes 294928 | tf_op jit(solution)/shard_map/reduce_scatter | solution.py:271
  986.7 72.0 %reduce-scatter.21.cloned.1.call-done = f32[96,768]{1,0:T(8,128)} async-done(((f32[768,768]{1,0:T(8,128)}), f32[96,768]{1,0:T(8,128)}) %reduce-scatter.21.cloned.1.call-update) | async-done | bytes 294928 | tf_op jit(solution)/shard_map/reduce_scatter | solution.py:270
  1058.7 140.1 %all-reduce.12.cloned.1.call-done = f32[128,4608]{1,0:T(8,128)} async-done(((f32[128,4608]{1,0:T(8,128)}), f32[128,4608]{1,0:T(8,128)}) %all-reduce.12.cloned.1.call-update) | async-done | bytes 2359312 | tf_op jit(solution)/shard_map/psum | solution.py:281
  (332 shorter events, 310.1 us)
Async XLA Ops:
  7.2 51.8 %copy-start.3 = (bf16[512,1,768]{2,0,1:T(8,128)(2,1)S(1)}, bf16[512,1,768]{2,0,1:T(8,128)(2,1)}, u32[]{:S(2)}) copy-start(bf16[512,1,768]{2,0,1:T(8,128)(2,1)} %param.17) | copy-start | bytes 2359300
  7.2 49.4 %all-gather.9.cloned.1.call-start = ((), (), s32[]{:S(2)}) async-start(), calls=%async_computation.8 | async-start | bytes 1327104 | tf_op jit(solution)/shard_map/all_gather | solution.py:73
  7.9 126.0 %all-gather.11.cloned.1.call-start = ((), (), s32[]{:S(2)}) async-start(), calls=%async_computation.9 | async-start | bytes 3932160 | tf_op jit(solution)/shard_map/all_gather | solution.py:96
  59.0 253.7 %copy-start.37 = (f32[768]{0:T(1024)}, f32[768]{0:T(1024)S(1)}, u32[]{:S(2)}) copy-start(f32[768]{0:T(1024)S(1)} %get-tuple-element.319) | copy-start | bytes 9220
  60.3 252.4 %reduce-scatter.13.cloned.1.call-start = ((), (), s32[]{:S(2)}) async-start(), calls=%async_computation.10 | async-start | bytes 7864320 | tf_op jit(solution)/shard_map/reduce_scatter | solution.py:133
  255.3 100.8 %all-gather.15.cloned.1.call-start = ((), (), s32[]{:S(2)}) async-start(), calls=%async_computation.12 | async-start | bytes 1327104 | tf_op jit(solution)/shard_map/all_gather | solution.py:79
  255.9 129.6 %all-gather.13.cloned.1.call-start = ((), (), s32[]{:S(2)}) async-start(), calls=%async_computation.11 | async-start | bytes 3932160 | tf_op jit(solution)/shard_map/all_gather | solution.py:144
  316.6 112.3 %all-gather.17.cloned.1.call-start = ((), (), s32[]{:S(2)}) async-start(), calls=%async_computation.13 | async-start | bytes 1327104 | tf_op jit(solution)/shard_map/all_gather | solution.py:81
  317.2 141.2 %all-gather.19.cloned.1.call-start = ((), (), s32[]{:S(2)}) async-start(), calls=%async_computation.15 | async-start | bytes 3932160 | tf_op jit(solution)/shard_map/all_gather | solution.py:174
  318.9 180.2 %reduce-scatter.15.cloned.1.call-start = ((), (), s32[]{:S(2)}) async-start(), calls=%async_computation.14 | async-start | bytes 3932160 | tf_op jit(solution)/shard_map/reduce_scatter | solution.py:151
  437.8 122.3 %reduce-scatter.17.cloned.1.call-start = ((), (), s32[]{:S(2)}) async-start(), calls=%async_computation.16 | async-start | bytes 7864320 | tf_op jit(solution)/shard_map/reduce_scatter | solution.py:184
  474.1 124.1 %all-gather.21.cloned.1.call-start = ((), (), s32[]{:S(2)}) async-start(), calls=%async_computation.17 | async-start | bytes 3932160 | tf_op jit(solution)/shard_map/all_gather | solution.py:195
  569.5 214.0 %reduce-scatter.27.cloned.1.call-start = ((), (), s32[]{:S(2)}) async-start(), calls=%async_computation.23 | async-start | bytes 884736
  720.8 132.4 %reduce-scatter.25.cloned.1.call-start = ((), (), s32[]{:S(2)}) async-start(), calls=%async_computation.22 | async-start | bytes 2211840
  737.2 176.1 %reduce-scatter.19.cloned.1.call-start = ((), (), s32[]{:S(2)}) async-start(), calls=%async_computation.18 | async-start | bytes 7864320 | tf_op jit(solution)/shard_map/reduce_scatter | solution.py:258
  745.3 241.4 %reduce-scatter.23.cloned.1.call-start = ((), (), s32[]{:S(2)}) async-start(), calls=%async_computation.21 | async-start | bytes 2654208 | tf_op jit(solution)/shard_map/reduce_scatter | solution.py:271
  754.7 304.0 %reduce-scatter.21.cloned.1.call-start = ((), (), s32[]{:S(2)}) async-start(), calls=%async_computation.20 | async-start | bytes 2654208 | tf_op jit(solution)/shard_map/reduce_scatter | solution.py:270
  761.0 152.3 %copy-start.4 = (bf16[512,1,768]{2,0,1:T(8,128)(2,1)S(1)}, bf16[512,1,768]{2,0,1:T(8,128)(2,1)}, u32[]{:S(2)}) copy-start(bf16[512,1,768]{2,0,1:T(8,128)(2,1)} %param.17) | copy-start | bytes 2359300
  761.0 152.3 %copy-start.31 = (f32[768]{0:T(1024)S(1)}, f32[768]{0:T(1024)}, u32[]{:S(2)}) copy-start(f32[768]{0:T(1024)} %copy-done.30) | copy-start | bytes 9220
  761.0 152.3 %copy-start.33 = (f32[768]{0:T(1024)S(1)}, f32[768]{0:T(1024)}, u32[]{:S(2)}) copy-start(f32[768]{0:T(1024)} %copy-done.32) | copy-start | bytes 9220
  761.0 152.3 %copy-start.35 = (f32[512]{0:T(512)S(1)}, f32[512]{0:T(512)}, u32[]{:S(2)}) copy-start(f32[512]{0:T(512)} %copy-done.34) | copy-start | bytes 6148
  761.1 437.7 %all-reduce.12.cloned.1.call-start = ((), (), s32[]{:S(2)}) async-start(), calls=%async_computation.19 | async-start | bytes 4718592 | tf_op jit(solution)/shard_map/psum | solution.py:281
  854.4 60.9 %copy-start.45 = (f32[512]{0:T(512)S(1)}, f32[512]{0:T(512)}, u32[]{:S(2)}) copy-start(f32[512]{0:T(512)} %copy-done.44) | copy-start | bytes 6148
  854.4 60.9 %copy-start.41 = (f32[512]{0:T(512)S(1)}, f32[512]{0:T(512)}, u32[]{:S(2)}) copy-start(f32[512]{0:T(512)} %copy-done.40) | copy-start | bytes 6148
  (58 other events, 228.0 us)
Sparse Core Ops, SparseCore 0:
  10.2 44.0 all-gather.8
  60.4 25.7 all-gather.10
  255.4 57.2 reduce-scatter.12
  315.0 41.0 all-gather.14
  358.2 27.2 all-gather.12
  387.8 41.0 all-gather.16
  431.1 27.2 all-gather.18
  461.1 37.9 reduce-scatter.14
  501.7 58.3 reduce-scatter.16
  569.6 28.5 all-gather.20
  720.9 62.4 reduce-scatter.26
  787.4 65.8 reduce-scatter.24
  855.9 57.2 reduce-scatter.18
  917.2 69.4 reduce-scatter.22
  990.6 68.0 reduce-scatter.20
  1064.7 134.0 all-reduce.11
where the time goes:
time: 1210 us
  waiting for transfers between devices  643 us (53%)
  blocking collectives  175 us (14%)
  matrix products  160 us (13%)
  other arithmetic  77 us (6%)
  local copies, waits for them, and re-layouts  61.4 us (5%)
  Pallas kernels  58.6 us (5%)
  between operations  16.6 us (1%)
  loops' own time  15.9 us (1%)
    psum x1, waiting for transfers between devices, shards(): lax.psum((local_squares, cond_table, d_ada_w, d_ada_b, d_gain_one, d_gain...  140 us
    unnamed x18, waiting for transfers between devices  89.6 us
    reduce_scatter x1, waiting for transfers between devices, shards(): lax.psum_scatter(grad_up, 'dp', scatter_dimension=0, tiled=True)  72 us
    reduce_scatter x1, waiting for transfers between devices, shards(): lax.psum_scatter(jnp.einsum('lbf,df->lbd', portion, up_w, preferred_eleme...  60.9 us
    dot_general x4, Pallas kernels, forward_block(): jnp.einsum('hqk,hke->hqe', probs, value_seq, preferred_element_type=jnp.f...  58.6 us
    reduce_scatter x1, waiting for transfers between devices, shards(): lax.psum_scatter(jnp.einsum('lbje,jde->lbd', portion, qkv_w, preferred_el...  58.1 us
    reduce_scatter x1, waiting for transfers between devices, shards(): lax.psum_scatter(jnp.einsum('lbe,ed->lbd', portion, out_w, preferred_elem...  56.3 us
    psum x1, blocking collectives, shards(): lax.psum((local_squares, cond_table, d_ada_w, d_ada_b, d_gain_one, d_gain...  41.4 us
  transfers between devices with their start and end apart: 16, of which 14 were waited for; matrix products, arithmetic and copies ran while one was open for 9% of the time, Pallas kernels for 0%

commit v1 on v0

--- a/solution.py
+++ b/solution.py
@@ -192,7 +192,36 @@
     d_middle = out_grad + middle_part
     d_gate_attn = jnp.sum(d_middle * attn_out, axis=0)
     d_attn = (gate_attn * d_middle).astype(jnp.bfloat16)
-    full_d_attn = lax.all_gather(d_attn, "tensor", axis=0, tiled=True)
+    local_part, r2, after = (
+        jax.lax.axis_size("tensor"),
+        jax.lax.axis_index("tensor"),
+        d_attn.shape[0],
+    )
+    in_order = tuple(
+        (t * local_part if hop_no == 0 else t for hop_no, t in enumerate(d_attn.shape))
+    )
+    state_next = y1 = d_attn
+    full_d_attn = lax.dynamic_update_slice_in_dim(
+        jnp.zeros(in_order, d_attn.dtype), d_attn, r2 * after, axis=0
+    )
+    for u in range(1, local_part // 2 + 1):
+        state_next = jax.lax.ppermute(
+            state_next,
+            "tensor",
+            perm=tuple(((hop_no, (hop_no + 1) % local_part) for hop_no in range(local_part))),
+        )
+        full_d_attn = lax.dynamic_update_slice_in_dim(
+            full_d_attn, state_next, (r2 - u) % local_part * after, axis=0
+        )
+        if 2 * u < local_part:
+            y1 = jax.lax.ppermute(
+                y1,
+                axis_name="tensor",
+                perm=tuple(((hop_no, (hop_no - 1) % local_part) for hop_no in range(local_part))),
+            )
+            full_d_attn = lax.dynamic_update_slice_in_dim(
+                full_d_attn, y1, (r2 + u) % local_part * after, axis=0
+            )
     grad_out = jnp.einsum("lbe,lbd->ed", mixed_all, full_d_attn, preferred_element_type=jnp.float32)
     d_mixed = jnp.einsum(
         "lbd,ed->lbe", full_d_attn, out_w, preferred_element_type=jnp.float32

time: 1210 us -> 1220 us (level)
    unnamed x18 -> x17, waiting for transfers between devices: 89.6 us -> 127 us
    reduce_scatter x1, waiting for transfers between devices: 58.1 us -> 22.9 us  [shards(): lax.psum_scatter(jnp.einsum('lbje,jde->lbd', portion, qkv_w, preferred_el...]
    all_gather x1 -> x0, waiting for transfers between devices: 28.6 us -> none  [shards(): full_d_attn = lax.all_gather(d_attn, 'tensor', axis=0, tiled=True)]
    ppermute x0 -> x3, waiting for transfers between devices: none -> 27.3 us  [the longest x2 27.3 us: shards(): jax.lax.ppermute(state_next, 'tensor', perm=tuple(((hop_no, (hop_no + 1)...]
    unnamed x149 -> x145, local copies, waits for them, and re-layouts: 32.1 us -> 36.4 us
  transfers between devices with their start and end apart: 16 -> 18, of which waited for: 14 -> 15; matrix products, arithmetic and copies ran while one was open for 9% -> 9% of each run, Pallas kernels for 0% -> 0%
where the time goes in v1:
time: 1220 us
  waiting for transfers between devices  646 us (53%)
  blocking collectives  175 us (14%)
  matrix products  160 us (13%)
  other arithmetic  75.6 us (6%)
  local copies, waits for them, and re-layouts  67.4 us (6%)
  Pallas kernels  58.6 us (5%)
  between operations  16.5 us (1%)
  loops' own time  15.9 us (1%)
    psum x1, waiting for transfers between devices, shards(): lax.psum((local_squares, cond_table, d_ada_w, d_ada_b, d_gain_one, d_gain...  140 us
    unnamed x17, waiting for transfers between devices  127 us
    reduce_scatter x1, waiting for transfers between devices, shards(): lax.psum_scatter(grad_up, 'dp', scatter_dimension=0, tiled=True)  72 us
    reduce_scatter x1, waiting for transfers between devices, shards(): lax.psum_scatter(jnp.einsum('lbf,df->lbd', portion, up_w, preferred_eleme...  60.9 us
    dot_general x4, Pallas kernels, forward_block(): jnp.einsum('hqk,hke->hqe', probs, value_seq, preferred_element_type=jnp.f...  58.6 us
    reduce_scatter x1, waiting for transfers between devices, shards(): lax.psum_scatter(jnp.einsum('lbe,ed->lbd', portion, out_w, preferred_elem...  56.7 us
    psum x1, blocking collectives, shards(): lax.psum((local_squares, cond_table, d_ada_w, d_ada_b, d_gain_one, d_gain...  41.5 us
    unnamed x1, blocking collectives  39.8 us
  transfers between devices with their start and end apart: 18, of which 15 were waited for; matrix products, arithmetic and copies ran while one was open for 9% of the time, Pallas kernels for 0%

profile of v1, /device:TPU:0, one launch (start us, length us, event | category | flops | bytes accessed | tf_op | source)
XLA Modules:
  0.0 1219.3 jit_solution(15635840758009118727)
XLA Ops:
  13.9 39.8 %all-reduce.9 = (bf16[4608]{0:T(1024)(128)(2,1)S(1)}, bf16[768]{0:T(1024)(128)(2,1)S(1)}, bf16[768]{0:T(1024)(128)(2,1)S(1)}, bf16[768]{0:T(1024)(128)(2,1)}) all-reduce(bf16[4608]{0:T(1024)(128)(2,1)S(1)} %dynamic-update-slice, bf16[768]{0:T(1024)(128)(2,1)S(1)} %dynamic-update-slice.1, ...), channel_id=1, replica_groups=mesh['dp'=8,'tensor'=4] {'dp'}, use_global_device_ids=true, to_apply=%add.4 | all-reduce | flops 6912 | bytes 27648
  60.7 34.3 %all_gather.43 = bf16[3,768,192]{2,0,1:T(4,128)(2,1)S(1)} all-gather(bf16[3,96,192]{2,0,1:T(4,128)(2,1)S(1)} %copy.49), channel_id=1, replica_groups=mesh['dp'=8,'tensor'=4] {'dp'}, dimensions={1}, use_global_device_ids=true | all-gather | bytes 995328 | tf_op jit(solution)/shard_map/all_gather | solution.py:76
  97.1 33.5 %all_gather.44 = bf16[192,768]{0,1:T(8,128)(2,1)} all-gather(bf16[192,96]{0,1:T(8,128)(2,1)S(1)} %copy.55), channel_id=1, replica_groups=mesh['dp'=8,'tensor'=4] {'dp'}, dimensions={1}, use_global_device_ids=true | all-gather | bytes 331776 | tf_op jit(solution)/shard_map/all_gather | solution.py:77
  146.4 101.9 %while.30 = (s32[]{:T(128)}, bf16[4,3,512,64]{3,2,1,0:T(8,128)(2,1)}, f32[4,3,512]{2,1,0:T(4,128)}, s32[4]{0:T(128)S(1)}, bf16[1,3,2048,64]{2,3,1,0:T(8,128)(2,1...) while((s32[]{:T(128)}, ...), condition=%wide.region_5.6_spmd, body=%wide.region_2.5_spmd.sunk | while | flops 1217493504 | bytes 29923640 | solution.py:128
  150.8 14.7 %dot_general.129 = f32[3,512,64]{2,1,0:T(8,128)} custom-call(bf16[3,512,64]{2,1,0:T(8,128)(2,1)} %bitcast.232, bf16[3,2048,64]{2,1,0:T(8,128)(2,1)S(1)} %bitcast.228, bf16[3,2048,64]{2,1,0:T(8,128)(2,1)} %bitcast.231), custom_call_target="tpu_custom_call" | custom-call | flops 805306368 | bytes 1769472 | tf_op jit(solution)/shard_map/while/body/eval_jaxpr/hqk,hke->hqe/dot_general | solution.py:125
  176.3 14.7 %dot_general.129 = f32[3,512,64]{2,1,0:T(8,128)} custom-call(bf16[3,512,64]{2,1,0:T(8,128)(2,1)} %bitcast.232, bf16[3,2048,64]{2,1,0:T(8,128)(2,1)S(1)} %bitcast.228, bf16[3,2048,64]{2,1,0:T(8,128)(2,1)} %bitcast.231), custom_call_target="tpu_custom_call" | custom-call | flops 805306368 | bytes 1769472 | tf_op jit(solution)/shard_map/while/body/eval_jaxpr/hqk,hke->hqe/dot_general | solution.py:125
  201.8 14.7 %dot_general.129 = f32[3,512,64]{2,1,0:T(8,128)} custom-call(bf16[3,512,64]{2,1,0:T(8,128)(2,1)} %bitcast.232, bf16[3,2048,64]{2,1,0:T(8,128)(2,1)S(1)} %bitcast.228, bf16[3,2048,64]{2,1,0:T(8,128)(2,1)} %bitcast.231), custom_call_target="tpu_custom_call" | custom-call | flops 805306368 | bytes 1769472 | tf_op jit(solution)/shard_map/while/body/eval_jaxpr/hqk,hke->hqe/dot_general | solution.py:125
  227.2 14.7 %dot_general.129 = f32[3,512,64]{2,1,0:T(8,128)} custom-call(bf16[3,512,64]{2,1,0:T(8,128)(2,1)} %bitcast.232, bf16[3,2048,64]{2,1,0:T(8,128)(2,1)S(1)} %bitcast.228, bf16[3,2048,64]{2,1,0:T(8,128)(2,1)} %bitcast.231), custom_call_target="tpu_custom_call" | custom-call | flops 805306368 | bytes 1769472 | tf_op jit(solution)/shard_map/while/body/eval_jaxpr/hqk,hke->hqe/dot_general | solution.py:125
  256.1 56.7 %reduce-scatter.13.cloned.1.call-done = f32[512,1,768]{2,0,1:T(8,128)} async-done(((f32[2048,1,768]{2,0,1:T(8,128)}), f32[512,1,768]{2,0,1:T(8,128)}) %reduce-scatter.13.cloned.1.call-update) | async-done | bytes 1572880 | tf_op jit(solution)/shard_map/reduce_scatter | solution.py:133
  320.4 26.1 %all-gather = bf16[8,1,384]{2,1,0:T(2,128)(2,1)S(1)} all-gather(bf16[1,1,384]{2,1,0:T(2,128)(2,1)S(1)} %reshape.572), channel_id=1, replica_groups=mesh['dp'=8,'tensor'=4] {'dp'}, dimensions={0}, use_global_device_ids=true | all-gather | bytes 6912 | tf_op jit(solution)/shard_map/all_gather | solution.py:80
  356.1 29.4 %all-gather.12.cloned.1.call-done = bf16[2048,1,768]{2,0,1:T(8,128)(2,1)} async-done(((bf16[512,1,768]{2,0,1:T(8,128)(2,1)}), bf16[2048,1,768]{2,0,1:T(8,128)(2,1)}) %all-gather.12.cloned.1.call-update) | async-done | bytes 3145744 | tf_op jit(solution)/shard_map/all_gather | solution.py:144
  393.0 35.9 %all-gather.16.cloned.1.call-done = bf16[768,768]{0,1:T(8,128)(2,1)} async-done(((bf16[768,96]{0,1:T(8,128)(2,1)}), bf16[768,768]{0,1:T(8,128)(2,1)}) %all-gather.16.cloned.1.call-update) | async-done | bytes 1179664 | tf_op jit(solution)/shard_map/all_gather | solution.py:81
  437.9 20.6 %all-gather.18.cloned.1.call-done = bf16[2048,1,768]{2,0,1:T(8,128)(2,1)} async-done(((bf16[512,1,768]{2,0,1:T(8,128)(2,1)}), bf16[2048,1,768]{2,0,1:T(8,128)(2,1)}) %all-gather.18.cloned.1.call-update) | async-done | bytes 3145744 | tf_op jit(solution)/shard_map/all_gather | solution.py:174
  475.6 23.6 %reduce-scatter.15.cloned.1.call-done = bf16[512,1,768]{2,0,1:T(8,128)(2,1)} async-done(((bf16[2048,1,768]{2,0,1:T(8,128)(2,1)}), bf16[512,1,768]{2,0,1:T(8,128)(2,1)}) %reduce-scatter.15.cloned.1.call-update) | async-done | bytes 786448 | tf_op jit(solution)/shard_map/reduce_scatter | solution.py:151
  499.1 60.9 %reduce-scatter.17.cloned.1.call-done = f32[512,1,768]{2,0,1:T(8,128)} async-done(((f32[2048,1,768]{2,0,1:T(8,128)}), f32[512,1,768]{2,0,1:T(8,128)}) %reduce-scatter.17.cloned.1.call-update) | async-done | bytes 1572880 | tf_op jit(solution)/shard_map/reduce_scatter | solution.py:184
  572.7 17.7 %collective-permute-done = bf16[512,1,768]{2,0,1:T(8,128)(2,1)S(1)} collective-permute-done((bf16[512,1,768]{2,0,1:T(8,128)(2,1)}, bf16[512,1,768]{2,0,1:T(8,128)(2,1)S(1)}, u32[]{:S(2)}, u32[]{:S(2)}) %collective-permute-start) | collective-permute-done | bytes 786464 | tf_op jit(solution)/shard_map/ppermute | solution.py:208
  608.3 110.2 %while.31 = (s32[]{:T(128)}, f32[1,3,2048,64]{2,3,1,0:T(8,128)S(1)}, f32[1,3,2048,64]{2,3,1,0:T(8,128)}, f32[4,3,512,64]{2,3,1,0:T(8,128)}, s32[4]{0:T(128)S(1)}...) while((s32[]{:T(128)}, ...), condition=%wide.region_15.16_spmd, body=%wide.region_13.15_spmd.sunk | while | flops 2042362368 | bytes 129411448 | solution.py:266
  766.3 22.9 %reduce-scatter.19.cloned.1.call-done = f32[512,1,768]{2,0,1:T(8,128)} async-done(((f32[2048,1,768]{2,0,1:T(8,128)}), f32[512,1,768]{2,0,1:T(8,128)}) %reduce-scatter.19.cloned.1.call-update) | async-done | bytes 1572880 | tf_op jit(solution)/shard_map/reduce_scatter | solution.py:287
  798.2 56.8 %reduce-scatter.27.cloned.1.call-done = f32[96,192]{1,0:T(8,128)} async-done(((f32[768,192]{1,0:T(8,128)}), f32[96,192]{1,0:T(8,128)}) %reduce-scatter.27.cloned.1.call-update) | async-done | bytes 73744
  856.7 67.8 %reduce-scatter.25.cloned.1.call-done = f32[96,576]{1,0:T(8,128)} async-done(((f32[768,576]{1,0:T(8,128)}), f32[96,576]{1,0:T(8,128)}) %reduce-scatter.25.cloned.1.call-update) | async-done | bytes 221200
  931.8 41.5 %all-reduce.8 = (f32[8,128]{1,0:T(8,128)S(1)}, f32[4608]{0:T(1024)}, f32[768]{0:T(1024)}, f32[768]{0:T(1024)}, f32[3072]{0:T(1024)}, /*index=5*/f32[768]{0:T(1024)}, f32[3]{0:T(128)S(1)}) all-reduce(f32[8,128]{1,0:T(8,128)S(1)} %dynamic_update_slice.50, f32[4608]{0:T(1024)S(1)} %reduce.25, ...), channel_id=1, replica_groups=mesh['dp'=8,'tensor'=4] {'dp','tensor'}, use_global_device_ids=true, to_apply=%region_25.26 | all-reduce | flops 11011 | bytes 88088 | tf_op jit(solution)/shard_map/psum | solution.py:310
  974.3 22.7 %reduce-scatter.23.cloned.1.call-done = f32[768,96]{0,1:T(8,128)} async-done(((f32[768,768]{0,1:T(8,128)}), f32[768,96]{0,1:T(8,128)}) %reduce-scatter.23.cloned.1.call-update) | async-done | bytes 294928 | tf_op jit(solution)/shard_map/reduce_scatter | solution.py:300
  997.0 72.0 %reduce-scatter.21.cloned.1.call-done = f32[96,768]{1,0:T(8,128)} async-done(((f32[768,768]{1,0:T(8,128)}), f32[96,768]{1,0:T(8,128)}) %reduce-scatter.21.cloned.1.call-update) | async-done | bytes 294928 | tf_op jit(solution)/shard_map/reduce_scatter | solution.py:299
  1069.0 140.1 %all-reduce.12.cloned.1.call-done = f32[128,4608]{1,0:T(8,128)} async-done(((f32[128,4608]{1,0:T(8,128)}), f32[128,4608]{1,0:T(8,128)}) %all-reduce.12.cloned.1.call-update) | async-done | bytes 2359312 | tf_op jit(solution)/shard_map/psum | solution.py:310
  (335 shorter events, 326.1 us)
Async XLA Ops:
  7.2 49.4 %copy-start.57 = (bf16[1,128]{1,0:T(2,128)(2,1)S(1)}, bf16[1,128]{1,0:T(2,128)(2,1)}, u32[]{:S(2)}) copy-start(bf16[1,128]{1,0:T(2,128)(2,1)} %param.18) | copy-start | bytes 772
  7.2 51.8 %copy-start.3 = (bf16[512,1,768]{2,0,1:T(8,128)(2,1)S(1)}, bf16[512,1,768]{2,0,1:T(8,128)(2,1)}, u32[]{:S(2)}) copy-start(bf16[512,1,768]{2,0,1:T(8,128)(2,1)} %param.17) | copy-start | bytes 2359300
  7.2 49.4 %all-gather.8.cloned.1.call-start = ((), (), s32[]{:S(2)}) async-start(), calls=%async_computation.8 | async-start | bytes 1327104 | tf_op jit(solution)/shard_map/all_gather | solution.py:73
  7.9 125.7 %all-gather.10.cloned.1.call-start = ((), (), s32[]{:S(2)}) async-start(), calls=%async_computation.9 | async-start | bytes 3932160 | tf_op jit(solution)/shard_map/all_gather | solution.py:96
  59.0 508.2 %copy-start.38 = (f32[768]{0:T(1024)}, f32[768]{0:T(1024)S(1)}, u32[]{:S(2)}) copy-start(f32[768]{0:T(1024)S(1)} %get-tuple-element.319) | copy-start | bytes 9220
  60.3 252.4 %reduce-scatter.13.cloned.1.call-start = ((), (), s32[]{:S(2)}) async-start(), calls=%async_computation.10 | async-start | bytes 7864320 | tf_op jit(solution)/shard_map/reduce_scatter | solution.py:133
  97.1 36.5 %copy-start.25 = (bf16[3,768,192]{1,2,0:T(8,128)(2,1)S(1)}, bf16[3,768,192]{1,2,0:T(8,128)(2,1)}, u32[]{:S(2)}) copy-start(bf16[3,768,192]{1,2,0:T(8,128)(2,1)} %copy.50) | copy-start | bytes 2654212
  255.0 101.1 %all-gather.14.cloned.1.call-start = ((), (), s32[]{:S(2)}) async-start(), calls=%async_computation.12 | async-start | bytes 1327104 | tf_op jit(solution)/shard_map/all_gather | solution.py:79
  255.6 129.9 %all-gather.12.cloned.1.call-start = ((), (), s32[]{:S(2)}) async-start(), calls=%async_computation.11 | async-start | bytes 3932160 | tf_op jit(solution)/shard_map/all_gather | solution.py:144
  316.6 112.2 %all-gather.16.cloned.1.call-start = ((), (), s32[]{:S(2)}) async-start(), calls=%async_computation.13 | async-start | bytes 1327104 | tf_op jit(solution)/shard_map/all_gather | solution.py:81
  317.2 141.2 %all-gather.18.cloned.1.call-start = ((), (), s32[]{:S(2)}) async-start(), calls=%async_computation.15 | async-start | bytes 3932160 | tf_op jit(solution)/shard_map/all_gather | solution.py:174
  319.6 179.5 %reduce-scatter.15.cloned.1.call-start = ((), (), s32[]{:S(2)}) async-start(), calls=%async_computation.14 | async-start | bytes 3932160 | tf_op jit(solution)/shard_map/reduce_scatter | solution.py:151
  437.8 122.2 %reduce-scatter.17.cloned.1.call-start = ((), (), s32[]{:S(2)}) async-start(), calls=%async_computation.16 | async-start | bytes 7864320 | tf_op jit(solution)/shard_map/reduce_scatter | solution.py:184
  474.1 315.1 %reduce-scatter.19.cloned.1.call-start = ((), (), s32[]{:S(2)}) async-start(), calls=%async_computation.17 | async-start | bytes 7864320 | tf_op jit(solution)/shard_map/reduce_scatter | solution.py:287
  571.0 19.5 %collective-permute-start = (bf16[512,1,768]{2,0,1:T(8,128)(2,1)}, bf16[512,1,768]{2,0,1:T(8,128)(2,1)S(1)}, u32[]{:S(2)}, u32[]{:S(2)}) collective-permute-start(bf16[512,1,768]{2,0,1:T(8,128)(2,1)} %get-tuple-element.368), channel_id=1, source_target_pairs={{0,1},{1,2},{2,3},{3,0},{4,5},{5,6},{6,7},{7,4},{8,9},{9,10},{10,1... | collective-permute-start | bytes 2359304 | tf_op jit(solution)/shard_map/ppermute | solution.py:208
  571.0 20.4 %collective-permute-start.1 = (bf16[512,1,768]{2,0,1:T(8,128)(2,1)}, bf16[512,1,768]{2,0,1:T(8,128)(2,1)S(1)}, u32[]{:S(2)}, u32[]{:S(2)}) collective-permute-start(bf16[512,1,768]{2,0,1:T(8,128)(2,1)} %get-tuple-element.368), channel_id=1, source_target_pairs={{0,3},{1,0},{2,1},{3,2},{4,7},{5,4},{6,5},{7,6},{8,11},{9,8},{10,9... | collective-permute-start | bytes 2359304 | tf_op jit(solution)/shard_map/ppermute | solution.py:217
  590.5 11.4 collective-permute-start.2
  730.9 124.1 %reduce-scatter.27.cloned.1.call-start = ((), (), s32[]{:S(2)}) async-start(), calls=%async_computation.22 | async-start | bytes 884736
  736.2 188.3 %reduce-scatter.25.cloned.1.call-start = ((), (), s32[]{:S(2)}) async-start(), calls=%async_computation.21 | async-start | bytes 2211840
  748.5 248.5 %reduce-scatter.23.cloned.1.call-start = ((), (), s32[]{:S(2)}) async-start(), calls=%async_computation.20 | async-start | bytes 2654208 | tf_op jit(solution)/shard_map/reduce_scatter | solution.py:300
  758.7 310.3 %reduce-scatter.21.cloned.1.call-start = ((), (), s32[]{:S(2)}) async-start(), calls=%async_computation.19 | async-start | bytes 2654208 | tf_op jit(solution)/shard_map/reduce_scatter | solution.py:299
  765.7 26.7 %copy-start.13 = (f32[512,1,768]{2,0,1:T(8,128)S(1)}, f32[512,1,768]{2,0,1:T(8,128)}, u32[]{:S(2)}) copy-start(f32[512,1,768]{2,0,1:T(8,128)} %reduce-scatter.13.cloned.1.call-done) | copy-start | bytes 4718596
  765.7 443.4 %all-reduce.12.cloned.1.call-start = ((), (), s32[]{:S(2)}) async-start(), calls=%async_computation.18 | async-start | bytes 4718592 | tf_op jit(solution)/shard_map/psum | solution.py:310
  797.4 129.0 %copy-start.14 = (f32[512,1,768]{2,0,1:T(8,128)S(1)}, f32[512,1,768]{2,0,1:T(8,128)}, u32[]{:S(2)}) copy-start(f32[512,1,768]{2,0,1:T(8,128)} %get-tuple-element.380) | copy-start | bytes 4718596
  (58 other events, 281.7 us)
Sparse Core Ops, SparseCore 0:
  10.2 44.0 all-gather.7
  60.4 25.7 all-gather.9
  255.1 57.5 reduce-scatter.12
  315.0 41.0 all-gather.13
  358.2 27.2 all-gather.11
  387.8 41.0 all-gather.15
  431.1 27.2 all-gather.17
  461.1 37.9 reduce-scatter.14
  501.7 58.3 reduce-scatter.16
  731.0 58.0 reduce-scatter.18
  792.5 62.5 reduce-scatter.26
  858.8 65.6 reduce-scatter.24
  928.6 68.4 reduce-scatter.22
  1001.0 67.9 reduce-scatter.20
  1075.0 134.1 all-reduce.11
